TPU v7x, 32 devices: a whole 2x2x4 slice. The times are simulated.
32 devices in a mesh: view: 4 (over y, x), blk: 8 (over z, core).
Axes of the slice: x: 2, y: 2, z: 4, core: 2. Of those that a mesh axis runs over, the one named last changes fastest.
Arguments:
- estimate: float32 [384, 64, 256], P('blk'), may hold values from 0.5 to 2
- views_seen: float32 [4, 384, 64, 256], P('view', 'blk'), may hold values from 0.2 to 5
- weight_mask: int32 [4, 384, 64, 256], P('view', 'blk'), may hold values from 1 to 3
- psf: float32 [4, 3, 21], P('view'), may hold values from 0.05 to 1
Outputs:
- joined: float32 [384, 64, 256], P('blk')
All inputs are finite; a program needn't handle non-finite values.
Results may differ from a plain program's by a relative error of at most 0.0001.
Values sent between devices are 32-bit elements; how exact they have to be, the bound alone decides.
A program may use at most 128 MiB of HBM per device.

v0:
```python
import jax
import jax.numpy as jnp
from jax import lax
from jax.sharding import PartitionSpec as P

ITERS = 2


def extended(cells, sides, width):
    for axis, dim in sides:
        count = lax.axis_size(axis)
        ends = count - 1
        head = lax.slice_in_dim(cells, 0, width, axis=dim)
        tail = lax.slice_in_dim(cells, cells.shape[dim] - width, cells.shape[dim], axis=dim)
        cells = jnp.concatenate(
            [
                lax.ppermute(tail, axis, [(i, (i + 1) % count) for i in range(ends)]),
                cells,
                lax.ppermute(head, axis, [((i + 1) % count, i) for i in range(ends)]),
            ],
            axis=dim,
        )
    return cells


def band_matrix(kernel, out_count, in_count, offset_by):
    row_index = jnp.arange(out_count)[:, None]
    col_index = jnp.arange(in_count)[None, :]
    offset_table = col_index - row_index + offset_by
    matches = offset_table[:, :, None] == jnp.arange(kernel.shape[0])[None, None, :]
    return jnp.sum(jnp.where(matches, kernel[None, None, :], 0.0), axis=-1)


def sweep_first(padded, kernel, count):
    result = kernel[0] * padded[0:count]
    for tap in range(1, kernel.shape[0]):
        result = result + kernel[tap] * padded[tap : tap + count]
    return result


def sweep_rest(volume, kernel):
    radius = (kernel.shape[-1] - 1) // 2
    along_y = band_matrix(kernel[1], volume.shape[1], volume.shape[1], radius)
    volume = jnp.einsum("ij,xjz->xiz", along_y, volume, precision=lax.Precision.HIGHEST)
    along_z = band_matrix(kernel[2], volume.shape[2], volume.shape[2], radius)
    return jnp.einsum("xyj,kj->xyk", volume, along_z, precision=lax.Precision.HIGHEST)


def body(estimate, views_seen, weight_mask, psf):
    slab = estimate.shape[0]
    radius = (psf.shape[-1] - 1) // 2
    normed = psf / jnp.sum(psf, axis=-1, keepdims=True)
    flipped = normed[:, :, ::-1]
    weights_all = lax.psum(jnp.sum(weight_mask.astype(jnp.float32), axis=0), "view")
    for iteration in range(ITERS):
        padded = extended(estimate, (("blk", 0),), radius)
        forward = normed[0]
        backward = flipped[0]
        blurred = sweep_rest(sweep_first(padded, forward[0], slab), forward)
        quotient = views_seen[0] / blurred
        quotient_wide = extended(quotient, (("blk", 0),), radius)
        correction = sweep_rest(sweep_first(quotient_wide, backward[0], slab), backward)
        numerator = weight_mask[0].astype(jnp.float32) * correction
        summed = lax.psum(numerator, "view")
        estimate = estimate * summed / weights_all
    return estimate


def solution(mesh):
    placed = (
        P("blk", None, None),
        P("view", "blk", None, None),
        P("view", "blk", None, None),
        P("view", None, None),
    )
    return jax.shard_map(
        body, mesh=mesh, in_specs=placed, out_specs=P("blk", None, None), check_vma=False
    )
```

profile of v0, /device:TPU:0, one launch (start us, length us, event | category | flops | bytes accessed | tf_op | source)
XLA Modules:
  0.0 507.7 jit_solution(5480964015441795965)
XLA Ops:
  6.5 0.0 all-reduce.6.cloned.1.call-start
  6.5 2.6 fusion.403
  9.1 3.2 collective-permute-start
  12.3 1.3 collective-permute-start.1
  13.6 0.8 reduce_sum.43
  14.4 0.8 broadcast_divide_fusion
  15.2 0.7 fusion.404
  15.9 0.6 fusion.405
  16.5 0.1 slice.671
  16.6 0.1 slice.672
  16.7 0.2 select_reduce_fusion.2
  17.0 1.0 select_reduce_fusion
  17.9 0.0 copy-start.6
  17.9 0.0 collective-permute-done
  18.0 1.2 constant_dynamic-update-slice_fusion.1
  19.2 0.0 copy-done.1
  19.2 0.5 constant_dynamic-update-slice_fusion
  19.7 0.0 copy-start.7
  19.7 0.0 collective-permute-done.1
  19.7 1.6 constant_dynamic-update-slice_fusion.2
  21.4 0.2 copy-done.7
  21.5 30.9 %fusion.244 = f32[48,256,64]{1,2,0:T(8,128)} fusion(f32[58,64,256]{2,1,0:T(8,128)S(1)} %constant_dynamic-update-slice_fusion.2, f32[58,64,256]{2,1,0:T(8,128)} %copy-done.7, f32[48,64,256]{2,1,0:T(8,128)S(1)} %copy-done.1, f32[]{:T(128)} %bitcast.22, f32[]{:T(128)} %bitcast.21, f32[]{:T(128)} %bitcast.20, f32[]{:T(128)} %bitcast.19, f32[]{:T(128)} %bitcast.18, ...), kind=kOutput, calls=%fused_computation.302 | convolution fusion | flops 636223488 | bytes 69249536 | tf_op jit(solution)/shard_map/ij,xjz->xiz/dot_general | solution.py:44
  52.4 0.0 copy-done.6
  52.4 0.0 copy-start
  52.4 5.9 %bitcast_divide_fusion.1 = f32[48,64,256]{2,1,0:T(8,128)S(1)} fusion(f32[1,48,64,256]{3,2,1,0:T(8,128)} %param.5, f32[48,256,64]{1,2,0:T(8,128)} %fusion.244, f32[256,256]{1,0:T(8,128)S(1)} %get-tuple-element.6), kind=kOutput, calls=%fused_computation.350 | convolution fusion | flops 2416705536 | bytes 9699328 | tf_op jit(solution)/shard_map/xyj,kj->xyk/dot_general | solution.py:46
  58.3 0.0 copy-start.5
  58.3 0.1 fusion.402
  58.4 8.0 %collective-permute-start.2 = (f32[10,64,256]{2,1,0:T(8,128)S(1)}, f32[10,64,256]{2,1,0:T(8,128)S(1)}, u32[]{:S(2)}, u32[]{:S(2)}) collective-permute-start(f32[10,64,256]{2,1,0:T(8,128)S(1)} %get-tuple-element.15), channel_id=1, source_target_pairs={{0,1},{1,2},{2,3},{3,4},{4,5},{5,6},{6,7},{8,9},{9,10},{10,11},{11... | collective-permute-start | bytes 1966088 | tf_op jit(solution)/shard_map/ppermute | solution.py:17
  66.4 1.5 collective-permute-start.3
  67.9 0.0 copy-done
  67.9 2.0 convert_bitcast_fusion
  69.9 0.0 copy-done.5
  69.9 0.0 collective-permute-done.2
  69.9 0.4 collective-permute-done.3
  70.4 0.4 copy-done.9
  70.8 0.8 copy-done.11
  71.6 44.5 %fusion.154 = f32[48,256,64]{1,2,0:T(8,128)} fusion(f32[48,64,256]{2,1,0:T(8,128)} %copy-done.5, f32[10,64,256]{2,1,0:T(8,128)} %copy-done.11, f32[10,64,256]{2,1,0:T(8,128)} %copy-done.9, f32[]{:T(128)} %bitcast.22, f32[]{:T(128)} %bitcast.21, f32[]{:T(128)} %bitcast.20, f32[]{:T(128)} %bitcast.19, f32[]{:T(128)} %bitcast.18, f32[]{:T(128)} %bitcast.17, ...), kind=kOutput, calls=%fused_computation.229 | convolution fusion | flops 651952128 | bytes 7618644 | tf_op jit(solution)/shard_map/ij,xjz->xiz/dot_general | solution.py:44
  116.1 6.2 %fusion.295 = f32[48,64,256]{2,1,0:T(8,128)} fusion(f32[48,256,64]{1,2,0:T(8,128)} %fusion.154, f32[256,256]{1,0:T(8,128)S(1)} %get-tuple-element.5, s32[1,48,64,256]{3,2,1,0:T(8,128)S(1)} %copy-done), kind=kOutput, calls=%fused_computation.358 | convolution fusion | flops 2417491968 | bytes 9699328 | tf_op jit(solution)/shard_map/xyj,kj->xyk/dot_general | solution.py:46
  122.4 0.0 all-reduce.6.cloned.1.call-update
  122.4 0.0 all-reduce.4.cloned.1.call-start
  122.4 146.7 %all-reduce.6.cloned.1.call-done = (f32[48,64,256]{2,1,0:T(8,128)}, f32[48,64,256]{2,1,0:T(8,128)}) async-done(((f32[48,64,256]{2,1,0:T(8,128)}, f32[48,64,256]{2,1,0:T(8,128)}), (f32[48,64,256]{2,1,0:T(8,128)}, f32[48,64,256]{2,1,0:T(8,128)})) %all-reduce.6.cloned.1.call-update) | async-done | bytes 6291472 | tf_op jit(solution)/shard_map/psum | solution.py:54
  269.1 4.7 multiply_divide_fusion.1
  273.8 0.0 copy-start.2
  273.8 1.7 copy-done.2
  275.4 0.1 fusion.401
  275.6 1.8 collective-permute-start.4
  277.4 1.5 collective-permute-start.5
  278.9 0.1 collective-permute-done.4
  279.0 0.8 copy-done.10
  279.9 2.8 collective-permute-done.5
  282.7 45.2 %fusion.79 = f32[48,256,64]{1,2,0:T(8,128)} fusion(f32[48,64,256]{2,1,0:T(8,128)} %copy-done.2, f32[10,64,256]{2,1,0:T(8,128)} %collective-permute-done.5, f32[10,64,256]{2,1,0:T(8,128)} %copy-done.10, f32[]{:T(128)} %bitcast.22, f32[]{:T(128)} %bitcast.21, f32[]{:T(128)} %bitcast.20, f32[]{:T(128)} %bitcast.19, f32[]{:T(128)} %bitcast.18, f32[]{:T(128)} %bitcast.17, ...), kind=kOutput, calls=%fused_computation.172 | convolution fusion | flops 651952128 | bytes 7618644 | tf_op jit(solution)/shard_map/ij,xjz->xiz/dot_general | solution.py:44
  327.9 5.8 %bitcast_divide_fusion = f32[48,64,256]{2,1,0:T(8,128)S(1)} fusion(f32[1,48,64,256]{3,2,1,0:T(8,128)} %param.5, f32[48,256,64]{1,2,0:T(8,128)} %fusion.79, f32[256,256]{1,0:T(8,128)} %copy-done.6), kind=kOutput, calls=%fused_computation.349 | convolution fusion | flops 2416705536 | bytes 9699328 | tf_op jit(solution)/shard_map/xyj,kj->xyk/dot_general | solution.py:46
  333.7 0.0 copy-start.4
  333.7 0.1 fusion.400
  333.8 10.3 %collective-permute-start.6 = (f32[10,64,256]{2,1,0:T(8,128)S(1)}, f32[10,64,256]{2,1,0:T(8,128)S(1)}, u32[]{:S(2)}, u32[]{:S(2)}) collective-permute-start(f32[10,64,256]{2,1,0:T(8,128)S(1)} %get-tuple-element.11), channel_id=1, source_target_pairs={{0,1},{1,2},{2,3},{3,4},{4,5},{5,6},{6,7},{8,9},{9,10},{10,11},{11... | collective-permute-start | bytes 1966088 | tf_op jit(solution)/shard_map/ppermute | solution.py:17
  344.2 1.6 collective-permute-start.7
  345.7 0.1 collective-permute-done.6
  345.8 0.9 copy-done.8
  346.7 1.6 collective-permute-done.7
  348.3 46.7 %fusion.4 = f32[48,256,64]{1,2,0:T(8,128)} fusion(f32[48,64,256]{2,1,0:T(8,128)} %copy-done.4, f32[10,64,256]{2,1,0:T(8,128)} %collective-permute-done.7, f32[10,64,256]{2,1,0:T(8,128)} %copy-done.8, f32[]{:T(128)} %bitcast.22, f32[]{:T(128)} %bitcast.21, f32[]{:T(128)} %bitcast.20, f32[]{:T(128)} %bitcast.19, f32[]{:T(128)} %bitcast.18, f32[]{:T(128)} %bitcast.17, ...), kind=kOutput, calls=%fused_computation.115 | convolution fusion | flops 651952128 | bytes 7618644 | tf_op jit(solution)/shard_map/ij,xjz->xiz/dot_general | solution.py:44
  395.0 6.2 %fusion.298 = f32[48,64,256]{2,1,0:T(8,128)} fusion(f32[48,256,64]{1,2,0:T(8,128)} %fusion.4, f32[256,256]{1,0:T(8,128)S(1)} %get-tuple-element.5, s32[1,48,64,256]{3,2,1,0:T(8,128)S(1)} %copy-done), kind=kOutput, calls=%fused_computation.359 | convolution fusion | flops 2417491968 | bytes 9699328 | tf_op jit(solution)/shard_map/xyj,kj->xyk/dot_general | solution.py:46
  401.2 0.0 all-reduce.4.cloned.1.call-update
  401.2 94.0 %all-reduce.4.cloned.1.call-done = f32[48,64,256]{2,1,0:T(8,128)} async-done(((f32[48,64,256]{2,1,0:T(8,128)}), f32[48,64,256]{2,1,0:T(8,128)}) %all-reduce.4.cloned.1.call-update) | async-done | bytes 3145744 | tf_op jit(solution)/shard_map/psum | solution.py:64
  495.2 5.7 %multiply_divide_fusion = f32[48,64,256]{2,1,0:T(8,128)} fusion(f32[48,64,256]{2,1,0:T(8,128)} %get-tuple-element.9, f32[48,64,256]{2,1,0:T(8,128)S(1)} %copy-done.3, f32[48,64,256]{2,1,0:T(8,128)} %all-reduce.4.cloned.1.call-done), kind=kLoop, calls=%fused_computation.351 | loop fusion | flops 1572864 | bytes 12582912 | tf_op jit(solution)/shard_map/div | solution.py:65
  (11 shorter events, 0.1 us)
Async XLA Ops:
  6.5 12.7 %copy-start.1 = (f32[48,64,256]{2,1,0:T(8,128)S(1)}, f32[48,64,256]{2,1,0:T(8,128)}, u32[]{:S(2)}) copy-start(f32[48,64,256]{2,1,0:T(8,128)} %param.4) | copy-start | bytes 9437188
  6.5 262.6 %all-reduce.6.cloned.1.call-start = ((), (), s32[]{:S(2)}) async-start(), calls=%async_computation.1 | async-start | bytes 12582912 | tf_op jit(solution)/shard_map/psum | solution.py:54
  9.1 8.8 %collective-permute-start = (f32[10,64,256]{2,1,0:T(8,128)}, f32[10,64,256]{2,1,0:T(8,128)}, u32[]{:S(2)}, u32[]{:S(2)}) collective-permute-start(f32[10,64,256]{2,1,0:T(8,128)} %get-tuple-element.19), channel_id=1, source_target_pairs={{0,1},{1,2},{2,3},{3,4},{4,5},{5,6},{6,7},{8,9},{9,10},{10,11},{11... | collective-permute-start | bytes 1966088 | tf_op jit(solution)/shard_map/ppermute | solution.py:17
  12.3 7.4 %collective-permute-start.1 = (f32[10,64,256]{2,1,0:T(8,128)}, f32[10,64,256]{2,1,0:T(8,128)}, u32[]{:S(2)}, u32[]{:S(2)}) collective-permute-start(f32[10,64,256]{2,1,0:T(8,128)} %get-tuple-element.20), channel_id=1, source_target_pairs={{1,0},{2,1},{3,2},{4,3},{5,4},{6,5},{7,6},{9,8},{10,9},{11,10},{12... | collective-permute-start | bytes 1966088 | tf_op jit(solution)/shard_map/ppermute | solution.py:19
  17.9 34.5 %copy-start.6 = (f32[256,256]{1,0:T(8,128)}, f32[256,256]{1,0:T(8,128)S(1)}, u32[]{:S(2)}) copy-start(f32[256,256]{1,0:T(8,128)S(1)} %get-tuple-element.6) | copy-start | bytes 786436
  19.7 1.8 copy-start.7
  52.4 15.4 %copy-start = (s32[1,48,64,256]{3,2,1,0:T(8,128)S(1)}, s32[1,48,64,256]{3,2,1,0:T(8,128)}, u32[]{:S(2)}) copy-start(s32[1,48,64,256]{3,2,1,0:T(8,128)} %param.6) | copy-start | bytes 9437188
  58.3 11.6 %copy-start.5 = (f32[48,64,256]{2,1,0:T(8,128)}, f32[48,64,256]{2,1,0:T(8,128)S(1)}, u32[]{:S(2)}) copy-start(f32[48,64,256]{2,1,0:T(8,128)S(1)} %bitcast_divide_fusion.1) | copy-start | bytes 9437188
  58.4 11.5 %collective-permute-start.2 = (f32[10,64,256]{2,1,0:T(8,128)S(1)}, f32[10,64,256]{2,1,0:T(8,128)S(1)}, u32[]{:S(2)}, u32[]{:S(2)}) collective-permute-start(f32[10,64,256]{2,1,0:T(8,128)S(1)} %get-tuple-element.15), channel_id=1, source_target_pairs={{0,1},{1,2},{2,3},{3,4},{4,5},{5,6},{6,7},{8,9},{9,10},{10,11},{11... | collective-permute-start | bytes 1966088 | tf_op jit(solution)/shard_map/ppermute | solution.py:17
  66.4 4.0 collective-permute-start.3
  69.9 0.8 copy-start.9
  70.7 0.8 copy-start.11
  122.4 372.8 %all-reduce.4.cloned.1.call-start = ((), (), s32[]{:S(2)}) async-start(), calls=%async_computation | async-start | bytes 6291456 | tf_op jit(solution)/shard_map/psum | solution.py:64
  273.8 1.7 copy-start.2
  275.6 3.5 collective-permute-start.4
  277.4 5.3 %collective-permute-start.5 = (f32[10,64,256]{2,1,0:T(8,128)S(1)}, f32[10,64,256]{2,1,0:T(8,128)}, u32[]{:S(2)}, u32[]{:S(2)}) collective-permute-start(f32[10,64,256]{2,1,0:T(8,128)S(1)} %get-tuple-element.14), channel_id=1, source_target_pairs={{1,0},{2,1},{3,2},{4,3},{5,4},{6,5},{7,6},{9,8},{10,9},{11,10},{12... | collective-permute-start | bytes 1966088 | tf_op jit(solution)/shard_map/ppermute | solution.py:19
  279.0 0.8 copy-start.10
  333.7 12.1 %copy-start.4 = (f32[48,64,256]{2,1,0:T(8,128)}, f32[48,64,256]{2,1,0:T(8,128)S(1)}, u32[]{:S(2)}) copy-start(f32[48,64,256]{2,1,0:T(8,128)S(1)} %bitcast_divide_fusion) | copy-start | bytes 9437188
  333.8 12.0 %collective-permute-start.6 = (f32[10,64,256]{2,1,0:T(8,128)S(1)}, f32[10,64,256]{2,1,0:T(8,128)S(1)}, u32[]{:S(2)}, u32[]{:S(2)}) collective-permute-start(f32[10,64,256]{2,1,0:T(8,128)S(1)} %get-tuple-element.11), channel_id=1, source_target_pairs={{0,1},{1,2},{2,3},{3,4},{4,5},{5,6},{6,7},{8,9},{9,10},{10,11},{11... | collective-permute-start | bytes 1966088 | tf_op jit(solution)/shard_map/ppermute | solution.py:17
  344.2 4.1 collective-permute-start.7
  345.8 0.9 copy-start.8
  401.2 94.0 %copy-start.3 = (f32[48,64,256]{2,1,0:T(8,128)S(1)}, f32[48,64,256]{2,1,0:T(8,128)}, u32[]{:S(2)}) copy-start(f32[48,64,256]{2,1,0:T(8,128)} %copy-done.2) | copy-start | bytes 9437188
Sparse Core Ops, SparseCore 0:
  122.5 146.5 all-reduce.5
  401.3 93.7 all-reduce.3
where the time goes:
time: 509 us; the launch traced here: 508 us
  waiting for transfers between devices  246 us (48%)
  matrix products  191 us (38%)
  starting transfers between devices  29.1 us (6%)
  other arithmetic  15.2 us (3%)
  between operations  13.7 us (3%)
  local copies, waits for them, and re-layouts  12.6 us (2%)
    dot_general x4, matrix products, sweep_rest(): jnp.einsum('ij,xjz->xiz', along_y, volume, precision=lax.Precision.HIGHEST)  167 us
    psum x1, waiting for transfers between devices, body(): lax.psum(jnp.sum(weight_mask.astype(jnp.float32), axis=0), 'view')  147 us
    psum x1, waiting for transfers between devices, body(): summed = lax.psum(numerator, 'view')  94 us
    dot_general x4, matrix products, sweep_rest(): jnp.einsum('xyj,kj->xyk', volume, along_z, precision=lax.Precision.HIGHEST)  24.1 us
    ppermute x4, starting transfers between devices, extended(): lax.ppermute(tail, axis, [(i, (i + 1) % count) for i in range(ends)])  23.3 us
    div x2, other arithmetic, body(): estimate = estimate * summed / weights_all  10.4 us
  transfers between devices with their start and end apart: 10, of which 7 were waited for; matrix products, arithmetic and copies ran while one was open for 2% of the time, Pallas kernels for 0%

commit v1 on v0

--- a/solution.py
+++ b/solution.py
@@ -47,11 +47,15 @@
 
 
 def body(estimate, views_seen, weight_mask, psf):
+
+    def shape_the_views(matrix, link_axis):
+        return jax.lax.all_gather(matrix, link_axis).sum(axis=0)
+
     slab = estimate.shape[0]
     radius = (psf.shape[-1] - 1) // 2
     normed = psf / jnp.sum(psf, axis=-1, keepdims=True)
     flipped = normed[:, :, ::-1]
-    weights_all = lax.psum(jnp.sum(weight_mask.astype(jnp.float32), axis=0), "view")
+    weights_all = shape_the_views(jnp.sum(weight_mask.astype(jnp.float32), axis=0), "view")
     for iteration in range(ITERS):
         padded = extended(estimate, (("blk", 0),), radius)
         forward = normed[0]

time: 509 us -> 466 us (0.916)
  waiting for transfers between devices: 246 us -> 189 us
  other arithmetic: 15.2 us -> 23.6 us
    psum x1 -> x0, waiting for transfers between devices: 147 us -> none  [body(): lax.psum(jnp.sum(weight_mask.astype(jnp.float32), axis=0), 'view')]
    psum x1 -> x2, waiting for transfers between devices: 94 us -> 179 us  [body(): summed = lax.psum(numerator, 'view')]
    all_gather x0 -> x1, waiting for transfers between devices: none -> 8.52 us  [shape_the_views(): return jax.lax.all_gather(matrix, link_axis).sum(axis=0)]
    reduce_sum x0 -> x1, other arithmetic: none -> 7.95 us  [shape_the_views(): return jax.lax.all_gather(matrix, link_axis).sum(axis=0)]
  transfers between devices with their start and end apart: 10 -> 11, of which waited for: 7 -> 6; matrix products, arithmetic and copies ran while one was open for 2% -> 22% of each run, Pallas kernels for 0% -> 0%
where the time goes in v1:
time: 466 us; the launch traced here: 464 us
  matrix products  193 us (41%)
  waiting for transfers between devices  189 us (41%)
  starting transfers between devices  32.8 us (7%)
  other arithmetic  23.6 us (5%)
  between operations  13.3 us (3%)
  local copies, waits for them, and re-layouts  12.8 us (3%)
    psum x2, waiting for transfers between devices, body(): summed = lax.psum(numerator, 'view')  179 us
    dot_general x4, matrix products, sweep_rest(): jnp.einsum('ij,xjz->xiz', along_y, volume, precision=lax.Precision.HIGHEST)  169 us
    ppermute x4, starting transfers between devices, extended(): lax.ppermute(tail, axis, [(i, (i + 1) % count) for i in range(ends)])  27.6 us
    dot_general x4, matrix products, sweep_rest(): jnp.einsum('xyj,kj->xyk', volume, along_z, precision=lax.Precision.HIGHEST)  23.9 us
    div x2, other arithmetic, body(): estimate = estimate * summed / weights_all  10.4 us
  transfers between devices with their start and end apart: 11, of which 6 were waited for; matrix products, arithmetic and copies ran while one was open for 22% of the time, Pallas kernels for 0%

profile of v1, /device:TPU:0, one launch (start us, length us, event | category | flops | bytes accessed | tf_op | source)
XLA Modules:
  0.0 464.4 jit_solution(2979616020431682387)
XLA Ops:
  6.5 0.0 all-gather.2.cloned.1.call-start
  6.5 3.9 convert_element_type.8
  10.5 0.0 all-gather.2.cloned.1.call-update
  10.5 0.0 all-reduce.3.cloned.1.call-start
  10.5 1.8 copy-done.2
  12.4 1.2 fusion.401
  13.6 3.2 collective-permute-start
  16.8 1.3 collective-permute-start.1
  18.1 0.0 copy-done.8
  18.1 0.1 reduce_sum.51
  18.2 0.1 broadcast_divide_fusion
  18.3 0.7 fusion.402
  19.0 0.6 fusion.403
  19.6 0.1 slice.671
  19.7 0.1 slice.672
  19.8 0.2 select_reduce_fusion.2
  20.0 1.0 select_reduce_fusion
  21.0 0.0 copy-start.6
  21.0 0.0 collective-permute-done
  21.0 1.4 constant_dynamic-update-slice_fusion.1
  22.4 0.5 constant_dynamic-update-slice_fusion
  22.9 0.0 copy-start.7
  22.9 0.0 collective-permute-done.1
  22.9 1.7 constant_dynamic-update-slice_fusion.2
  24.7 0.1 copy-done.7
  24.7 30.9 %fusion.244 = f32[48,256,64]{1,2,0:T(8,128)} fusion(f32[58,64,256]{2,1,0:T(8,128)S(1)} %constant_dynamic-update-slice_fusion.2, f32[58,64,256]{2,1,0:T(8,128)} %copy-done.7, f32[48,64,256]{2,1,0:T(8,128)S(1)} %copy-done.2, f32[]{:T(128)} %bitcast.22, f32[]{:T(128)} %bitcast.21, f32[]{:T(128)} %bitcast.20, f32[]{:T(128)} %bitcast.19, f32[]{:T(128)} %bitcast.18, ...), kind=kOutput, calls=%fused_computation.302 | convolution fusion | flops 636223488 | bytes 69249536 | tf_op jit(solution)/shard_map/ij,xjz->xiz/dot_general | solution.py:44
  55.6 0.0 copy-done.6
  55.6 5.7 %bitcast_divide_fusion.1 = f32[48,64,256]{2,1,0:T(8,128)S(1)} fusion(f32[1,48,64,256]{3,2,1,0:T(8,128)} %param.5, f32[48,256,64]{1,2,0:T(8,128)} %fusion.244, f32[256,256]{1,0:T(8,128)S(1)} %get-tuple-element.6), kind=kOutput, calls=%fused_computation.350 | convolution fusion | flops 2416705536 | bytes 9699328 | tf_op jit(solution)/shard_map/xyj,kj->xyk/dot_general | solution.py:46
  61.4 0.1 fusion.400
  61.4 1.3 collective-permute-start.3
  62.7 10.3 %collective-permute-start.2 = (f32[10,64,256]{2,1,0:T(8,128)S(1)}, f32[10,64,256]{2,1,0:T(8,128)S(1)}, u32[]{:S(2)}, u32[]{:S(2)}) collective-permute-start(f32[10,64,256]{2,1,0:T(8,128)S(1)} %get-tuple-element.13), channel_id=1, source_target_pairs={{0,1},{1,2},{2,3},{3,4},{4,5},{5,6},{6,7},{8,9},{9,10},{10,11},{11... | collective-permute-start | bytes 1966088 | tf_op jit(solution)/shard_map/ppermute | solution.py:17
  73.1 0.0 collective-permute-done.3
  73.1 1.5 collective-permute-done.2
  74.5 0.0 copy-done.5
  74.6 0.8 copy-done.12
  75.4 45.7 %fusion.154 = f32[48,256,64]{1,2,0:T(8,128)} fusion(f32[48,64,256]{2,1,0:T(8,128)} %copy-done.5, f32[10,64,256]{2,1,0:T(8,128)} %copy-done.10, f32[10,64,256]{2,1,0:T(8,128)} %copy-done.12, f32[]{:T(128)} %bitcast.22, f32[]{:T(128)} %bitcast.21, f32[]{:T(128)} %bitcast.20, f32[]{:T(128)} %bitcast.19, f32[]{:T(128)} %bitcast.18, f32[]{:T(128)} %bitcast.17, ...), kind=kOutput, calls=%fused_computation.229 | convolution fusion | flops 651952128 | bytes 7618644 | tf_op jit(solution)/shard_map/ij,xjz->xiz/dot_general | solution.py:44
  121.1 6.2 %bitcast_multiply_fusion.1 = f32[48,64,256]{2,1,0:T(8,128)} fusion(f32[48,256,64]{1,2,0:T(8,128)} %fusion.154, f32[256,256]{1,0:T(8,128)S(1)} %get-tuple-element.5, s32[1,48,64,256]{3,2,1,0:T(8,128)S(1)} %copy-done), kind=kOutput, calls=%fused_computation.352 | convolution fusion | flops 2417491968 | bytes 9699328 | tf_op jit(solution)/shard_map/xyj,kj->xyk/dot_general | solution.py:46
  127.3 0.0 all-reduce.3.cloned.1.call-update
  127.3 0.0 all-reduce.5.cloned.1.call-start
  127.3 8.5 %all-gather.2.cloned.1.call-done = f32[4,48,64,256]{3,2,1,0:T(8,128)} async-done(((f32[1,48,64,256]{3,2,1,0:T(8,128)}), f32[4,48,64,256]{3,2,1,0:T(8,128)}) %all-gather.2.cloned.1.call-update) | async-done | bytes 12582928 | tf_op jit(solution)/shard_map/all_gather | solution.py:52
  135.9 8.0 %reduce_sum.62 = f32[48,64,256]{2,1,0:T(8,128)} reduce(f32[4,48,64,256]{3,2,1,0:T(8,128)} %all-gather.2.cloned.1.call-done, f32[]{:T(128)} %constant.2.clone.1), dimensions={0}, to_apply=%region_6.7 | reduce | flops 2359296 | bytes 15728644 | tf_op jit(solution)/shard_map/reduce_sum | solution.py:52
  143.8 82.4 %all-reduce.3.cloned.1.call-done = f32[48,64,256]{2,1,0:T(8,128)} async-done(((f32[48,64,256]{2,1,0:T(8,128)}), f32[48,64,256]{2,1,0:T(8,128)}) %all-reduce.3.cloned.1.call-update) | async-done | bytes 3145744 | tf_op jit(solution)/shard_map/psum | solution.py:68
  226.2 4.7 %multiply_divide_fusion.1 = f32[48,64,256]{2,1,0:T(8,128)S(1)} fusion(f32[48,64,256]{2,1,0:T(8,128)} %reduce_sum.62, f32[48,64,256]{2,1,0:T(8,128)} %param.4, f32[48,64,256]{2,1,0:T(8,128)} %all-reduce.3.cloned.1.call-done), kind=kLoop, calls=%fused_computation.356 | loop fusion | flops 1572864 | bytes 12582912 | tf_op jit(solution)/shard_map/div | solution.py:69
  230.9 1.6 copy-done.3
  232.5 0.1 fusion.399
  232.7 1.3 collective-permute-start.5
  234.0 3.9 collective-permute-start.4
  237.8 0.0 collective-permute-done.5
  237.8 0.9 copy-done.11
  238.7 0.1 collective-permute-done.4
  238.8 45.3 %fusion.79 = f32[48,256,64]{1,2,0:T(8,128)} fusion(f32[48,64,256]{2,1,0:T(8,128)} %copy-done.3, f32[10,64,256]{2,1,0:T(8,128)} %copy-done.11, f32[10,64,256]{2,1,0:T(8,128)} %collective-permute-done.4, f32[]{:T(128)} %bitcast.22, f32[]{:T(128)} %bitcast.21, f32[]{:T(128)} %bitcast.20, f32[]{:T(128)} %bitcast.19, f32[]{:T(128)} %bitcast.18, f32[]{:T(128)} %bitcast.17, ...), kind=kOutput, calls=%fused_computation.172 | convolution fusion | flops 651952128 | bytes 7618644 | tf_op jit(solution)/shard_map/ij,xjz->xiz/dot_general | solution.py:44
  284.1 5.8 %bitcast_divide_fusion = f32[48,64,256]{2,1,0:T(8,128)S(1)} fusion(f32[1,48,64,256]{3,2,1,0:T(8,128)} %param.5, f32[48,256,64]{1,2,0:T(8,128)} %fusion.79, f32[256,256]{1,0:T(8,128)} %copy-done.6), kind=kOutput, calls=%fused_computation.349 | convolution fusion | flops 2416705536 | bytes 9699328 | tf_op jit(solution)/shard_map/xyj,kj->xyk/dot_general | solution.py:46
  290.0 0.0 copy-start.4
  290.0 0.1 fusion.398
  290.1 1.3 collective-permute-start.7
  291.4 10.2 %collective-permute-start.6 = (f32[10,64,256]{2,1,0:T(8,128)S(1)}, f32[10,64,256]{2,1,0:T(8,128)}, u32[]{:S(2)}, u32[]{:S(2)}) collective-permute-start(f32[10,64,256]{2,1,0:T(8,128)S(1)} %get-tuple-element.9), channel_id=1, source_target_pairs={{0,1},{1,2},{2,3},{3,4},{4,5},{5,6},{6,7},{8,9},{9,10},{10,11},{11... | collective-permute-start | bytes 1966088 | tf_op jit(solution)/shard_map/ppermute | solution.py:17
  301.6 0.0 collective-permute-done.7
  301.6 0.8 copy-done.9
  302.4 0.1 collective-permute-done.6
  302.5 46.7 %fusion.4 = f32[48,256,64]{1,2,0:T(8,128)} fusion(f32[48,64,256]{2,1,0:T(8,128)} %copy-done.4, f32[10,64,256]{2,1,0:T(8,128)} %copy-done.9, f32[10,64,256]{2,1,0:T(8,128)} %collective-permute-done.6, f32[]{:T(128)} %bitcast.22, f32[]{:T(128)} %bitcast.21, f32[]{:T(128)} %bitcast.20, f32[]{:T(128)} %bitcast.19, f32[]{:T(128)} %bitcast.18, f32[]{:T(128)} %bitcast.17, ...), kind=kOutput, calls=%fused_computation.115 | convolution fusion | flops 651952128 | bytes 7618644 | tf_op jit(solution)/shard_map/ij,xjz->xiz/dot_general | solution.py:44
  349.3 6.2 %bitcast_multiply_fusion = f32[48,64,256]{2,1,0:T(8,128)} fusion(f32[48,256,64]{1,2,0:T(8,128)} %fusion.4, f32[256,256]{1,0:T(8,128)S(1)} %get-tuple-element.5, s32[1,48,64,256]{3,2,1,0:T(8,128)S(1)} %copy-done), kind=kOutput, calls=%fused_computation.351 | convolution fusion | flops 2417491968 | bytes 9699328 | tf_op jit(solution)/shard_map/xyj,kj->xyk/dot_general | solution.py:46
  355.5 0.0 all-reduce.5.cloned.1.call-update
  355.5 96.6 %all-reduce.5.cloned.1.call-done = f32[48,64,256]{2,1,0:T(8,128)} async-done(((f32[48,64,256]{2,1,0:T(8,128)}), f32[48,64,256]{2,1,0:T(8,128)}) %all-reduce.5.cloned.1.call-update) | async-done | bytes 3145744 | tf_op jit(solution)/shard_map/psum | solution.py:68
  452.1 5.7 %multiply_divide_fusion = f32[48,64,256]{2,1,0:T(8,128)} fusion(f32[48,64,256]{2,1,0:T(8,128)S(1)} %copy-done.1, f32[48,64,256]{2,1,0:T(8,128)} %copy-done.3, f32[48,64,256]{2,1,0:T(8,128)} %all-reduce.5.cloned.1.call-done), kind=kLoop, calls=%fused_computation.353 | loop fusion | flops 1572864 | bytes 12582912 | tf_op jit(solution)/shard_map/div | solution.py:69
  (17 shorter events, 0.1 us)
Async XLA Ops:
  6.5 129.3 %all-gather.2.cloned.1.call-start = ((), (), s32[]{:S(2)}) async-start(), calls=%async_computation.1 | async-start | bytes 15728640 | tf_op jit(solution)/shard_map/all_gather | solution.py:52
  10.5 1.9 copy-start.2
  10.5 7.6 %copy-start.8 = (f32[1,3,21]{2,0,1:T(1,128)S(1)}, f32[1,3,21]{2,0,1:T(1,128)}, u32[]{:S(2)}) copy-start(f32[1,3,21]{2,0,1:T(1,128)} %param.7) | copy-start | bytes 760
  10.5 215.7 %all-reduce.3.cloned.1.call-start = ((), (), s32[]{:S(2)}) async-start(), calls=%async_computation | async-start | bytes 6291456 | tf_op jit(solution)/shard_map/psum | solution.py:68
  13.6 7.4 %collective-permute-start = (f32[10,64,256]{2,1,0:T(8,128)}, f32[10,64,256]{2,1,0:T(8,128)}, u32[]{:S(2)}, u32[]{:S(2)}) collective-permute-start(f32[10,64,256]{2,1,0:T(8,128)} %get-tuple-element.17), channel_id=1, source_target_pairs={{0,1},{1,2},{2,3},{3,4},{4,5},{5,6},{6,7},{8,9},{9,10},{10,11},{11... | collective-permute-start | bytes 1966088 | tf_op jit(solution)/shard_map/ppermute | solution.py:17
  16.8 6.2 %collective-permute-start.1 = (f32[10,64,256]{2,1,0:T(8,128)}, f32[10,64,256]{2,1,0:T(8,128)}, u32[]{:S(2)}, u32[]{:S(2)}) collective-permute-start(f32[10,64,256]{2,1,0:T(8,128)} %get-tuple-element.18), channel_id=1, source_target_pairs={{1,0},{2,1},{3,2},{4,3},{5,4},{6,5},{7,6},{9,8},{10,9},{11,10},{12... | collective-permute-start | bytes 1966088 | tf_op jit(solution)/shard_map/ppermute | solution.py:19
  21.0 34.6 %copy-start.6 = (f32[256,256]{1,0:T(8,128)}, f32[256,256]{1,0:T(8,128)S(1)}, u32[]{:S(2)}) copy-start(f32[256,256]{1,0:T(8,128)S(1)} %get-tuple-element.6) | copy-start | bytes 786436
  22.9 1.8 copy-start.7
  61.3 13.2 %copy-start.5 = (f32[48,64,256]{2,1,0:T(8,128)}, f32[48,64,256]{2,1,0:T(8,128)S(1)}, u32[]{:S(2)}) copy-start(f32[48,64,256]{2,1,0:T(8,128)S(1)} %bitcast_divide_fusion.1) | copy-start | bytes 9437188
  61.4 11.6 %collective-permute-start.3 = (f32[10,64,256]{2,1,0:T(8,128)S(1)}, f32[10,64,256]{2,1,0:T(8,128)S(1)}, u32[]{:S(2)}, u32[]{:S(2)}) collective-permute-start(f32[10,64,256]{2,1,0:T(8,128)S(1)} %get-tuple-element.14), channel_id=1, source_target_pairs={{1,0},{2,1},{3,2},{4,3},{5,4},{6,5},{7,6},{9,8},{10,9},{11,10},{12... | collective-permute-start | bytes 1966088 | tf_op jit(solution)/shard_map/ppermute | solution.py:19
  62.7 11.8 %collective-permute-start.2 = (f32[10,64,256]{2,1,0:T(8,128)S(1)}, f32[10,64,256]{2,1,0:T(8,128)S(1)}, u32[]{:S(2)}, u32[]{:S(2)}) collective-permute-start(f32[10,64,256]{2,1,0:T(8,128)S(1)} %get-tuple-element.13), channel_id=1, source_target_pairs={{0,1},{1,2},{2,3},{3,4},{4,5},{5,6},{6,7},{8,9},{9,10},{10,11},{11... | collective-permute-start | bytes 1966088 | tf_op jit(solution)/shard_map/ppermute | solution.py:17
  73.1 1.5 copy-start.10
  74.6 0.8 copy-start.12
  75.4 45.7 %copy-start = (s32[1,48,64,256]{3,2,1,0:T(8,128)S(1)}, s32[1,48,64,256]{3,2,1,0:T(8,128)}, u32[]{:S(2)}) copy-start(s32[1,48,64,256]{3,2,1,0:T(8,128)} %param.6) | copy-start | bytes 9437188
  127.3 324.8 %all-reduce.5.cloned.1.call-start = ((), (), s32[]{:S(2)}) async-start(), calls=%async_computation.2 | async-start | bytes 6291456 | tf_op jit(solution)/shard_map/psum | solution.py:68
  230.9 1.7 copy-start.3
  232.7 5.2 %collective-permute-start.5 = (f32[10,64,256]{2,1,0:T(8,128)S(1)}, f32[10,64,256]{2,1,0:T(8,128)S(1)}, u32[]{:S(2)}, u32[]{:S(2)}) collective-permute-start(f32[10,64,256]{2,1,0:T(8,128)S(1)} %get-tuple-element.12), channel_id=1, source_target_pairs={{1,0},{2,1},{3,2},{4,3},{5,4},{6,5},{7,6},{9,8},{10,9},{11,10},{12... | collective-permute-start | bytes 1966088 | tf_op jit(solution)/shard_map/ppermute | solution.py:19
  234.0 4.9 %collective-permute-start.4 = (f32[10,64,256]{2,1,0:T(8,128)S(1)}, f32[10,64,256]{2,1,0:T(8,128)}, u32[]{:S(2)}, u32[]{:S(2)}) collective-permute-start(f32[10,64,256]{2,1,0:T(8,128)S(1)} %get-tuple-element.11), channel_id=1, source_target_pairs={{0,1},{1,2},{2,3},{3,4},{4,5},{5,6},{6,7},{8,9},{9,10},{10,11},{11... | collective-permute-start | bytes 1966088 | tf_op jit(solution)/shard_map/ppermute | solution.py:17
  237.8 0.9 copy-start.11
  290.0 11.6 %copy-start.4 = (f32[48,64,256]{2,1,0:T(8,128)}, f32[48,64,256]{2,1,0:T(8,128)S(1)}, u32[]{:S(2)}) copy-start(f32[48,64,256]{2,1,0:T(8,128)S(1)} %bitcast_divide_fusion) | copy-start | bytes 9437188
  290.1 11.5 %collective-permute-start.7 = (f32[10,64,256]{2,1,0:T(8,128)S(1)}, f32[10,64,256]{2,1,0:T(8,128)S(1)}, u32[]{:S(2)}, u32[]{:S(2)}) collective-permute-start(f32[10,64,256]{2,1,0:T(8,128)S(1)} %get-tuple-element.10), channel_id=1, source_target_pairs={{1,0},{2,1},{3,2},{4,3},{5,4},{6,5},{7,6},{9,8},{10,9},{11,10},{12... | collective-permute-start | bytes 1966088 | tf_op jit(solution)/shard_map/ppermute | solution.py:19
  291.4 11.2 %collective-permute-start.6 = (f32[10,64,256]{2,1,0:T(8,128)S(1)}, f32[10,64,256]{2,1,0:T(8,128)}, u32[]{:S(2)}, u32[]{:S(2)}) collective-permute-start(f32[10,64,256]{2,1,0:T(8,128)S(1)} %get-tuple-element.9), channel_id=1, source_target_pairs={{0,1},{1,2},{2,3},{3,4},{4,5},{5,6},{6,7},{8,9},{9,10},{10,11},{11... | collective-permute-start | bytes 1966088 | tf_op jit(solution)/shard_map/ppermute | solution.py:17
  301.6 0.8 copy-start.9
  355.5 96.6 %copy-start.1 = (f32[48,64,256]{2,1,0:T(8,128)S(1)}, f32[48,64,256]{2,1,0:T(8,128)}, u32[]{:S(2)}) copy-start(f32[48,64,256]{2,1,0:T(8,128)} %reduce_sum.62) | copy-start | bytes 9437188
Sparse Core Ops, SparseCore 0:
  10.6 125.2 all-gather.1
  139.0 87.2 all-reduce.2
  355.6 96.4 all-reduce.4
